TPU v7x, 32 devices: a whole 2x2x4 slice. The times are simulated.
32 devices in a mesh: dp: 8 (over z, y), group: 4 (over x, core).
Axes of the slice: x: 2, y: 2, z: 4, core: 2. Of those that a mesh axis runs over, the one named last changes fastest.
Arguments:
- gradients: float32 [32, 3, 320, 960], P(('dp', 'group')), may hold values from -0.8 to 0.8
- errors: bfloat16 [32, 3, 320, 960], P(('dp', 'group')), may hold values from -0.59765625 to 0.59765625
- q_init: float32 [3, 960, 32], replicated, may hold values from -0.1875 to 0.1875
- owners: int32 [3], replicated, may hold values from 0 to 31, as said below
- buckets: int32 [3], replicated, may hold values from 0 to 3
- learn_rates: float32 [4], replicated, may hold values from 0.2 to 1
- beta_values: float32 [4], replicated, may hold values from 0.5 to 0.95
- momentum: bfloat16 [64, 320, 960], P(('dp', 'group')), may hold values from -3 to 3
Outputs:
- new_errors: bfloat16 [32, 3, 320, 960], P(('dp', 'group'))
- weight_steps: bfloat16 [32, 3, 320, 960], P(('dp', 'group'))
- new_momentum: bfloat16 [64, 320, 960], P(('dp', 'group'))
Inputs may be any that keep to these rules, and one draw needn't show every extreme that they name: `owners`: no device owns more than 2 matrices, and some device owns exactly 2.
All inputs are finite; a program needn't handle non-finite values.
Results may differ from a plain program's by a relative error of at most 0.001.
Values may be sent and summed in bfloat16 or wider, within the bound.
No kernel may reach another device: no remote copies, remote signals or barrier semaphores. Data moves between devices by JAX's collectives and lax.ppermute only.
A program may use at most 64 MiB of HBM per device.

v0:
```python
import jax
import jax.numpy as jnp
from jax import lax
from jax.sharding import PartitionSpec as P


def from_root(value, axis, source):
    kept = jnp.where(lax.axis_index(axis) == source, value, 0).astype(value.dtype)
    return lax.psum(kept, axis)


def on_device(gradients, errors, q_init, owners, buckets, learn_rates, beta_values, momentum):
    highest = lax.Precision.HIGHEST
    slot_count = momentum.shape[0]
    mat_count = owners.shape[0]
    bucket_count = learn_rates.shape[0]
    my_index = lax.axis_index(("dp", "group"))
    positions = jnp.arange(mat_count, dtype=jnp.int32)
    earlier = (owners[None, :] == owners[:, None]) & (positions[None, :] < positions[:, None])
    slot_list = jnp.sum(earlier.astype(jnp.int32), axis=1)
    bucket_hits = buckets[:, None] == jnp.arange(bucket_count, dtype=jnp.int32)[None, :]
    rate_list = jnp.sum(jnp.where(bucket_hits, learn_rates[None, :], 0.0), axis=1)
    beta_list = jnp.sum(jnp.where(bucket_hits, beta_values[None, :], 0.0), axis=1)
    merged = gradients[0] + errors[0].astype(jnp.float32)
    p_local = jnp.einsum("mkd,mdr->mkr", merged, q_init, precision=highest)
    p_sum = lax.psum(p_local, ("dp", "group"))
    gram_matrix = jnp.einsum("mkr,mks->mrs", p_sum, p_sum, precision=highest)
    lower_factor = jnp.linalg.cholesky(gram_matrix)
    p_hat = lax.linalg.triangular_solve(
        lower_factor, p_sum, left_side=False, lower=True, transpose_a=True
    )
    q_local = jnp.einsum("mkd,mkr->mdr", merged, p_hat, precision=highest)
    q_sum = lax.psum(q_local, ("dp", "group"))
    approx = jnp.einsum("mkr,mdr->mkd", p_hat, q_local, precision=highest)
    new_errors = (merged - approx).astype(jnp.bfloat16)
    update = jnp.einsum("mkr,mdr->mkd", p_hat, q_sum, precision=highest)
    slot_range = jnp.arange(slot_count, dtype=jnp.int32)
    new_slab = jnp.zeros(momentum.shape, jnp.float32)
    step_list = []
    for matrix in range(mat_count):
        old_state = lax.dynamic_index_in_dim(momentum, slot_list[matrix], 0, keepdims=False).astype(
            jnp.float32
        )
        mom_new = beta_list[matrix] * old_state + update[matrix]
        step_value = (-rate_list[matrix] * (update[matrix] + beta_list[matrix] * mom_new)).astype(
            jnp.bfloat16
        )
        step_value = from_root(step_value, ("dp", "group"), owners[matrix])
        step_list.append(step_value)
        selected = (slot_range == slot_list[matrix]) & (owners[matrix] == my_index)
        new_slab = new_slab + jnp.where(selected[:, None, None], mom_new[None], 0.0)
    return (new_errors[None], jnp.stack(step_list)[None], new_slab.astype(jnp.bfloat16))


def solution(mesh):
    placed = (
        P(("dp", "group"), None, None, None),
        P(("dp", "group"), None, None, None),
        P(),
        P(),
        P(),
        P(),
        P(),
        P(("dp", "group"), None, None),
    )
    return jax.shard_map(
        on_device,
        mesh=mesh,
        in_specs=placed,
        out_specs=(
            P(("dp", "group"), None, None, None),
            P(("dp", "group"), None, None, None),
            P(("dp", "group"), None, None),
        ),
        check_vma=False,
    )
```

profile of v0, /device:TPU:0, one launch (start us, length us, event | category | flops | bytes accessed | tf_op | source)
XLA Modules:
  0.0 456.5 jit_solution(16836187007871859211)
XLA Ops:
  7.2 0.0 copy-start
  7.2 0.0 all-reduce.5.cloned.1.call-start
  7.2 0.9 copy-done
  8.2 7.3 %fusion.2 = f32[3,320,32]{1,2,0:T(8,128)} fusion(f32[3,960,32]{1,2,0:T(8,128)S(1)} %copy-done, f32[1,3,320,960]{3,2,1,0:T(8,128)} %param.8, bf16[1,3,320,960]{3,2,1,0:T(8,128)(2,1)} %param.9), kind=kOutput, calls=%fused_computation.3 | convolution fusion | flops 355737600 | bytes 6021120 | tf_op jit(solution)/shard_map/mkd,mdr->mkr/dot_general | solution.py:25
  15.5 0.0 all-reduce.5.cloned.1.call-update
  15.5 0.2 convert_reduce_fusion
  15.7 0.7 fusion.28
  20.2 0.6 fusion.29
  24.7 114.3 %all-reduce.5.cloned.1.call-done = f32[3,320,32]{1,2,0:T(8,128)} async-done(((f32[3,320,32]{1,2,0:T(8,128)}), f32[3,320,32]{1,2,0:T(8,128)}) %all-reduce.5.cloned.1.call-update) | async-done | bytes 122896 | tf_op jit(solution)/shard_map/psum | solution.py:26
  139.0 1.3 fusion.32
  140.3 0.1 copy.13
  140.4 8.8 %custom-call.7 = f32[3,32,32]{2,1,0:T(8,128)S(1)} custom-call(f32[3,32,32]{2,1,0:T(8,128)S(1)} %fusion.26), custom_call_target="Cholesky" | custom-call | tf_op jit(solution)/shard_map/jit(cholesky)/cholesky | solution.py:28
  149.2 0.1 compare_reduce_fusion
  149.3 0.1 select_bitcast_fusion
  149.4 7.4 %custom-call.8 = f32[3,1,32,32]{2,3,1,0:T(8,128)S(1)} custom-call(f32[3,1,32,32]{3,2,1,0:T(8,128)S(1)} %select_bitcast_fusion), custom_call_target="InvertDiagBlocksLowerTriangular" | custom-call | tf_op jit(solution)/shard_map/triangular_solve | solution.py:29
  156.8 1.3 fusion.24
  158.1 4.8 %fusion = f32[3,960,32]{1,2,0:T(8,128)S(1)} fusion(f32[3,320,32]{1,2,0:T(8,128)S(1)} %fusion.24, f32[1,3,320,960]{3,2,1,0:T(8,128)} %param.8, bf16[1,3,320,960]{3,2,1,0:T(8,128)(2,1)S(1)} %copy-done.2), kind=kOutput, calls=%fused_computation.1 | convolution fusion | flops 355737600 | bytes 6021120 | tf_op jit(solution)/shard_map/mkd,mkr->mdr/dot_general | solution.py:32
  162.9 6.3 %fusion.5 = bf16[1,3,320,960]{3,2,1,0:T(8,128)(2,1)} fusion(f32[3,320,32]{1,2,0:T(8,128)S(1)} %fusion.24, f32[3,960,32]{1,2,0:T(8,128)S(1)} %fusion, f32[1,3,320,960]{3,2,1,0:T(8,128)} %param.8, bf16[1,3,320,960]{3,2,1,0:T(8,128)(2,1)S(1)} %copy-done.2), kind=kOutput, calls=%fused_computation.9 | convolution fusion | flops 357580800 | bytes 7864320 | tf_op jit(solution)/shard_map/mkr,mdr->mkd/dot_general | solution.py:34
  169.3 0.7 all-reduce.7.cloned.1.call-update
  170.0 0.2 all-reduce.9.cloned.1.call-start
  170.2 0.2 select_reduce_fusion.2
  170.4 0.7 fusion.30
  174.9 130.5 %all-reduce.7.cloned.1.call-done = f32[3,960,32]{1,2,0:T(8,128)} async-done(((f32[3,960,32]{1,2,0:T(8,128)}), f32[3,960,32]{1,2,0:T(8,128)}) %all-reduce.7.cloned.1.call-update) | async-done | bytes 368656 | tf_op jit(solution)/shard_map/psum | solution.py:33
  305.4 4.3 fusion.33
  309.7 3.9 fusion.19
  313.6 0.0 all-reduce.9.cloned.1.call-update
  313.6 0.6 compare_and_fusion.2
  314.2 1.3 compare_and_fusion
  315.5 4.8 %add_bitcast_fusion.2 = (f32[320,960]{1,0:T(8,128)S(1)}, f32[320,960]{1,0:T(8,128)S(1)}, f32[320,960]{1,0:T(8,128)S(1)}) fusion(f32[3,320,960]{2,1,0:T(8,128)} %copy-done.1, f32[]{:T(128)} %bitcast.8, bf16[2,320,960]{2,1,0:T(8,128)(2,1)S(1)} %copy-done.3, s32[]{:T(128)S(6)} %select_n.55, s32[]{:T(128)S(6)} %select_n.58, f32[]{:T(128)} %bitcast.15, ...), kind=kLoop, calls=%fused_computation.27 | loop fusion | flops 2764800 | bytes 9216024 | tf_op jit(solution)/shard_map/jit(_where)/broadcast_in_dim | solution.py:51
  320.4 1.7 add_convert_fusion
  322.1 125.0 %all-reduce.9.cloned.1.call-done = (bf16[1,320,960]{2,1,0:T(8,128)(2,1)}, bf16[1,320,960]{2,1,0:T(8,128)(2,1)}, bf16[1,320,960]{2,1,0:T(8,128)(2,1)}) async-done(((bf16[1,320,960]{2,1,0:T(8,128)(2,1)}, bf16[1,320,960]{2,1,0:T(8,128)(2,1)}, bf16[1,320,960]{2,1,0:T(8,128)(2,1)}), (bf16[1,320,960]{2,1,0:T(8,128)(2,1)}, bf16[1,320,960]{2,1,0:T(8,128)(2,1)}, ...) | async-done | bytes 1843216 | tf_op jit(solution)/shard_map/psum | solution.py:9
  447.0 3.0 maximum_bitcast_fusion
  (21 shorter events, 0.1 us)
Async XLA Ops:
  7.2 1.0 copy-start
  7.2 8.3 %copy-start.5 = (s32[3]{0:T(128)S(1)}, s32[3]{0:T(128)}, u32[]{:S(2)}) copy-start(s32[3]{0:T(128)} %param.11) | copy-start | bytes 40
  7.2 131.8 %all-reduce.5.cloned.1.call-start = ((), (), s32[]{:S(2)}) async-start(), calls=%async_computation | async-start | bytes 294912 | tf_op jit(solution)/shard_map/psum | solution.py:26
  8.2 149.9 %copy-start.2 = (bf16[1,3,320,960]{3,2,1,0:T(8,128)(2,1)S(1)}, bf16[1,3,320,960]{3,2,1,0:T(8,128)(2,1)}, u32[]{:S(2)}) copy-start(bf16[1,3,320,960]{3,2,1,0:T(8,128)(2,1)} %param.9) | copy-start | bytes 5529604
  162.9 6.4 %copy-start.4 = (f32[3,960,32]{1,2,0:T(8,128)}, f32[3,960,32]{1,2,0:T(8,128)S(1)}, u32[]{:S(2)}) copy-start(f32[3,960,32]{1,2,0:T(8,128)S(1)} %fusion) | copy-start | bytes 1105924
  162.9 7.3 %copy-start.6 = (f32[4]{0:T(128)S(1)}, f32[4]{0:T(128)}, u32[]{:S(2)}) copy-start(f32[4]{0:T(128)} %param.13) | copy-start | bytes 52
  162.9 7.3 %copy-start.7 = (s32[3]{0:T(128)S(1)}, s32[3]{0:T(128)}, u32[]{:S(2)}) copy-start(s32[3]{0:T(128)} %param.12) | copy-start | bytes 40
  162.9 7.3 %copy-start.8 = (f32[4]{0:T(128)S(1)}, f32[4]{0:T(128)}, u32[]{:S(2)}) copy-start(f32[4]{0:T(128)} %param.14) | copy-start | bytes 52
  169.2 136.1 %all-reduce.7.cloned.1.call-start = ((), (), s32[]{:S(2)}) async-start(), calls=%async_computation.1 | async-start | bytes 786432 | tf_op jit(solution)/shard_map/psum | solution.py:33
  170.0 277.0 %all-reduce.9.cloned.1.call-start = ((), (), s32[]{:S(2)}) async-start(), calls=%async_computation.2 | async-start | bytes 3932160 | tf_op jit(solution)/shard_map/psum | solution.py:9
  174.9 134.8 %copy-start.3 = (bf16[2,320,960]{2,1,0:T(8,128)(2,1)S(1)}, bf16[2,320,960]{2,1,0:T(8,128)(2,1)}, u32[]{:S(2)}) copy-start(bf16[2,320,960]{2,1,0:T(8,128)(2,1)} %param.15) | copy-start | bytes 3686404
  309.7 3.9 copy-start.1
Sparse Core Ops, SparseCore 0:
  15.6 123.3 all-reduce.4
  175.9 129.3 all-reduce.6
  313.7 133.2 all-reduce.8
where the time goes:
time: 457 us
  waiting for transfers between devices  371 us (81%)
  other arithmetic  32.1 us (7%)
  between operations  25.4 us (6%)
  matrix products  25.2 us (6%)
    psum x1, waiting for transfers between devices, on_device(): q_sum = lax.psum(q_local, ('dp', 'group'))  131 us
    psum x1, waiting for transfers between devices, from_root(): return lax.psum(kept, axis)  125 us
    psum x1, waiting for transfers between devices, on_device(): p_sum = lax.psum(p_local, ('dp', 'group'))  114 us
  transfers between devices with their start and end apart: 3, of which 3 were waited for; matrix products, arithmetic and copies ran while one was open for 2% of the time, Pallas kernels for 0%

commit v1 on v0

--- a/solution.py
+++ b/solution.py
@@ -2,6 +2,12 @@
 import jax.numpy as jnp
 from jax import lax
 from jax.sharding import PartitionSpec as P
+
+
+def gather_and_add(x, mesh_axis):
+    shards = lax.all_gather(x, mesh_axis, axis=0, tiled=False)
+    summed = shards.sum(axis=0)
+    return summed
 
 
 def from_root(value, axis, source):
@@ -23,7 +29,7 @@
     beta_list = jnp.sum(jnp.where(bucket_hits, beta_values[None, :], 0.0), axis=1)
     merged = gradients[0] + errors[0].astype(jnp.float32)
     p_local = jnp.einsum("mkd,mdr->mkr", merged, q_init, precision=highest)
-    p_sum = lax.psum(p_local, ("dp", "group"))
+    p_sum = gather_and_add(p_local, ("dp", "group"))
     gram_matrix = jnp.einsum("mkr,mks->mrs", p_sum, p_sum, precision=highest)
     lower_factor = jnp.linalg.cholesky(gram_matrix)
     p_hat = lax.linalg.triangular_solve(

time: 457 us -> 398 us (0.87)
  waiting for transfers between devices: 371 us -> 310 us
    psum x1 -> x0, waiting for transfers between devices: 114 us -> none  [on_device(): p_sum = lax.psum(p_local, ('dp', 'group'))]
    all_gather x0 -> x1, waiting for transfers between devices: none -> 57.3 us  [gather_and_add(): shards = lax.all_gather(x, mesh_axis, axis=0, tiled=False)]
  transfers between devices with their start and end apart: 3 -> 3, of which waited for: 3 -> 3; matrix products, arithmetic and copies ran while one was open for 2% -> 3% of each run, Pallas kernels for 0% -> 0%
where the time goes in v1:
time: 398 us; the launch traced here: 397 us
  waiting for transfers between devices  310 us (78%)
  other arithmetic  34.9 us (9%)
  between operations  25.4 us (6%)
  matrix products  23.2 us (6%)
    psum x1, waiting for transfers between devices, on_device(): q_sum = lax.psum(q_local, ('dp', 'group'))  127 us
    psum x1, waiting for transfers between devices, from_root(): return lax.psum(kept, axis)  125 us
    all_gather x1, waiting for transfers between devices, gather_and_add(): shards = lax.all_gather(x, mesh_axis, axis=0, tiled=False)  57.3 us
    another operation x4, other arithmetic, on_device(): lower_factor = jnp.linalg.cholesky(gram_matrix)  8.96 us
  transfers between devices with their start and end apart: 3, of which 3 were waited for; matrix products, arithmetic and copies ran while one was open for 3% of the time, Pallas kernels for 0%

profile of v1, /device:TPU:0, one launch (start us, length us, event | category | flops | bytes accessed | tf_op | source)
XLA Modules:
  0.0 397.1 jit_solution(1436154054713227769)
XLA Ops:
  7.2 0.0 all-gather.3.cloned.1.call-start
  7.2 0.9 copy-done
  8.2 7.2 %fusion.2 = f32[3,320,32]{1,2,0:T(8,128)} fusion(f32[3,960,32]{1,2,0:T(8,128)S(1)} %copy-done, f32[1,3,320,960]{3,2,1,0:T(8,128)} %param.8, bf16[1,3,320,960]{3,2,1,0:T(8,128)(2,1)} %param.9), kind=kOutput, calls=%fused_computation.3 | convolution fusion | flops 355737600 | bytes 6021120 | tf_op jit(solution)/shard_map/mkd,mdr->mkr/dot_general | solution.py:31
  15.3 0.0 all-gather.3.cloned.1.call-update
  15.4 0.2 convert_reduce_fusion
  15.5 0.7 fusion.28
  20.0 0.6 fusion.29
  24.6 57.3 %all-gather.3.cloned.1.call-done = f32[96,320,32]{1,2,0:T(8,128)} async-done(((f32[3,320,32]{1,2,0:T(8,128)}), f32[96,320,32]{1,2,0:T(8,128)}) %all-gather.3.cloned.1.call-update) | async-done | bytes 3932176 | tf_op jit(solution)/shard_map/all_gather | solution.py:8
  81.8 2.8 reduce_sum.36
  84.7 0.3 fusion.32
  85.0 0.1 copy.15
  85.1 8.8 %custom-call.7 = f32[3,32,32]{2,1,0:T(8,128)S(1)} custom-call(f32[3,32,32]{2,1,0:T(8,128)S(1)} %fusion.26), custom_call_target="Cholesky" | custom-call | tf_op jit(solution)/shard_map/jit(cholesky)/cholesky | solution.py:34
  93.9 0.1 compare_reduce_fusion
  94.0 0.1 select_bitcast_fusion
  94.1 7.4 %custom-call.8 = f32[3,1,32,32]{2,3,1,0:T(8,128)S(1)} custom-call(f32[3,1,32,32]{3,2,1,0:T(8,128)S(1)} %select_bitcast_fusion), custom_call_target="InvertDiagBlocksLowerTriangular" | custom-call | tf_op jit(solution)/shard_map/triangular_solve | solution.py:35
  101.5 0.3 fusion.24
  101.8 4.8 %fusion = f32[3,960,32]{1,2,0:T(8,128)S(1)} fusion(f32[3,320,32]{1,2,0:T(8,128)S(1)} %fusion.24, f32[1,3,320,960]{3,2,1,0:T(8,128)} %param.8, bf16[1,3,320,960]{3,2,1,0:T(8,128)(2,1)S(1)} %copy-done.2), kind=kOutput, calls=%fused_computation.1 | convolution fusion | flops 355737600 | bytes 6021120 | tf_op jit(solution)/shard_map/mkd,mkr->mdr/dot_general | solution.py:38
  106.7 6.3 %fusion.5 = bf16[1,3,320,960]{3,2,1,0:T(8,128)(2,1)} fusion(f32[3,320,32]{1,2,0:T(8,128)S(1)} %fusion.24, f32[3,960,32]{1,2,0:T(8,128)S(1)} %fusion, f32[1,3,320,960]{3,2,1,0:T(8,128)} %param.8, bf16[1,3,320,960]{3,2,1,0:T(8,128)(2,1)S(1)} %copy-done.2), kind=kOutput, calls=%fused_computation.9 | convolution fusion | flops 357580800 | bytes 7864320 | tf_op jit(solution)/shard_map/mkr,mdr->mkd/dot_general | solution.py:40
  113.0 0.7 all-reduce.4.cloned.1.call-update
  113.8 0.2 all-reduce.6.cloned.1.call-start
  114.0 0.2 select_reduce_fusion.2
  114.2 0.7 fusion.30
  118.6 127.4 %all-reduce.4.cloned.1.call-done = f32[3,960,32]{1,2,0:T(8,128)} async-done(((f32[3,960,32]{1,2,0:T(8,128)}), f32[3,960,32]{1,2,0:T(8,128)}) %all-reduce.4.cloned.1.call-update) | async-done | bytes 368656 | tf_op jit(solution)/shard_map/psum | solution.py:39
  246.0 4.3 %fusion.33 = f32[3,320,960]{2,1,0:T(8,128)S(1)} fusion(f32[3,320,32]{1,2,0:T(8,128)S(1)} %fusion.24, f32[3,960,32]{1,2,0:T(8,128)} %all-reduce.4.cloned.1.call-done), kind=kOutput, calls=%fused_computation.60 | convolution fusion | flops 353894400 | bytes 4177920 | tf_op jit(solution)/shard_map/mkr,mdr->mkd/dot_general | solution.py:42
  250.3 3.9 fusion.19
  254.2 0.0 all-reduce.6.cloned.1.call-update
  254.2 0.6 compare_and_fusion.2
  254.9 1.3 compare_and_fusion
  256.2 4.8 %add_bitcast_fusion.2 = (f32[320,960]{1,0:T(8,128)S(1)}, f32[320,960]{1,0:T(8,128)S(1)}, f32[320,960]{1,0:T(8,128)S(1)}) fusion(f32[3,320,960]{2,1,0:T(8,128)} %copy-done.1, f32[]{:T(128)} %bitcast.9, bf16[2,320,960]{2,1,0:T(8,128)(2,1)S(1)} %copy-done.3, s32[]{:T(128)S(6)} %select_n.55, s32[]{:T(128)S(6)} %select_n.58, f32[]{:T(128)} %bitcast.16, ...), kind=kLoop, calls=%fused_computation.27 | loop fusion | flops 2764800 | bytes 9216024 | tf_op jit(solution)/shard_map/jit(_where)/broadcast_in_dim | solution.py:57
  261.0 1.7 add_convert_fusion
  262.7 124.9 %all-reduce.6.cloned.1.call-done = (bf16[1,320,960]{2,1,0:T(8,128)(2,1)}, bf16[1,320,960]{2,1,0:T(8,128)(2,1)}, bf16[1,320,960]{2,1,0:T(8,128)(2,1)}) async-done(((bf16[1,320,960]{2,1,0:T(8,128)(2,1)}, bf16[1,320,960]{2,1,0:T(8,128)(2,1)}, bf16[1,320,960]{2,1,0:T(8,128)(2,1)}), (bf16[1,320,960]{2,1,0:T(8,128)(2,1)}, bf16[1,320,960]{2,1,0:T(8,128)(2,1)}, ...) | async-done | bytes 1843216 | tf_op jit(solution)/shard_map/psum | solution.py:15
  387.6 3.0 maximum_bitcast_fusion
  (22 shorter events, 0.1 us)
Async XLA Ops:
  7.2 1.0 copy-start
  7.2 8.2 %copy-start.5 = (s32[3]{0:T(128)S(1)}, s32[3]{0:T(128)}, u32[]{:S(2)}) copy-start(s32[3]{0:T(128)} %param.11) | copy-start | bytes 40
  7.2 74.7 %all-gather.3.cloned.1.call-start = ((), (), s32[]{:S(2)}) async-start(), calls=%async_computation.1 | async-start | bytes 4866048 | tf_op jit(solution)/shard_map/all_gather | solution.py:8
  81.8 20.0 %copy-start.2 = (bf16[1,3,320,960]{3,2,1,0:T(8,128)(2,1)S(1)}, bf16[1,3,320,960]{3,2,1,0:T(8,128)(2,1)}, u32[]{:S(2)}) copy-start(bf16[1,3,320,960]{3,2,1,0:T(8,128)(2,1)} %param.9) | copy-start | bytes 5529604
  106.6 6.4 %copy-start.4 = (f32[3,960,32]{1,2,0:T(8,128)}, f32[3,960,32]{1,2,0:T(8,128)S(1)}, u32[]{:S(2)}) copy-start(f32[3,960,32]{1,2,0:T(8,128)S(1)} %fusion) | copy-start | bytes 1105924
  106.6 7.3 %copy-start.6 = (f32[4]{0:T(128)S(1)}, f32[4]{0:T(128)}, u32[]{:S(2)}) copy-start(f32[4]{0:T(128)} %param.13) | copy-start | bytes 52
  106.7 7.3 %copy-start.7 = (s32[3]{0:T(128)S(1)}, s32[3]{0:T(128)}, u32[]{:S(2)}) copy-start(s32[3]{0:T(128)} %param.12) | copy-start | bytes 40
  106.7 7.3 %copy-start.8 = (f32[4]{0:T(128)S(1)}, f32[4]{0:T(128)}, u32[]{:S(2)}) copy-start(f32[4]{0:T(128)} %param.14) | copy-start | bytes 52
  113.0 133.0 %all-reduce.4.cloned.1.call-start = ((), (), s32[]{:S(2)}) async-start(), calls=%async_computation | async-start | bytes 786432 | tf_op jit(solution)/shard_map/psum | solution.py:39
  113.8 273.9 %all-reduce.6.cloned.1.call-start = ((), (), s32[]{:S(2)}) async-start(), calls=%async_computation.2 | async-start | bytes 3932160 | tf_op jit(solution)/shard_map/psum | solution.py:15
  118.6 131.7 %copy-start.3 = (bf16[2,320,960]{2,1,0:T(8,128)(2,1)S(1)}, bf16[2,320,960]{2,1,0:T(8,128)(2,1)}, u32[]{:S(2)}) copy-start(bf16[2,320,960]{2,1,0:T(8,128)(2,1)} %param.15) | copy-start | bytes 3686404
  250.3 3.9 copy-start.1
Sparse Core Ops, SparseCore 0:
  15.5 66.3 all-gather.2
  119.7 126.2 all-reduce.3
  254.4 133.2 all-reduce.5
